TPU v7x, 32 devices: a whole 2x2x4 slice. The times are simulated.
32 devices in a mesh: groups: 2 (over y), dp: 4 (over x, core), tensor: 4 (over z).
Axes of the slice: x: 2, y: 2, z: 4, core: 2. Of those that a mesh axis runs over, the one named last changes fastest.
Arguments:
- query: bfloat16 [4096, 512], P(('groups', 'dp'), 'tensor'), parts along dimension 0, may hold values from -4.5 to 4.5
- keys: bfloat16 [4096, 512], P(('groups', 'dp'), 'tensor'), parts along dimension 0, may hold values from -4.5 to 4.5
- values: bfloat16 [4096, 512], P(('groups', 'dp'), 'tensor'), parts along dimension 0, may hold values from -6 to 6
- upstream: bfloat16 [4096, 8192], P(('groups', 'dp', 'tensor')), parts along dimension 0, may hold values from -6 to 6
- projection: bfloat16 [512, 8192], P('tensor', 'dp'), may hold values from -0.0625 to 0.0625
- lengths: int32 [8, 8], P(('groups', 'dp')), parts along dimension 0, may hold values from 1 to 256, 512 in all within a row
Outputs:
- grad_query: bfloat16 [4096, 512], P(('groups', 'dp'), 'tensor'), parts along dimension 0
- grad_keys: bfloat16 [4096, 512], P(('groups', 'dp'), 'tensor'), parts along dimension 0
- grad_values: bfloat16 [4096, 512], P(('groups', 'dp'), 'tensor'), parts along dimension 0
- grad_projection: float32 [1024, 8192], P(('groups', 'tensor'), 'dp'), parts along dimension 0
There are 2 independent parts, one for each index of `groups`. A program takes and returns all parts, laid end to end along the dimension named above; an argument that names none is the same for every part. Nothing has to cross between parts.
Inputs may be any that keep to these rules, and one draw needn't show every extreme that they name: Each row holds the lengths of the 8 documents of one sequence in order; they sum to 512 and the largest is exactly 256.
All inputs are finite; a program needn't handle non-finite values.
Results may differ from a plain program's by a relative error of at most 0.014.
Values may be sent and summed in bfloat16 or wider, within the bound.
No kernel may reach another device: no remote copies, remote signals or barrier semaphores. Data moves between devices by JAX's collectives and lax.ppermute only.
A program may use at most 64 MiB of HBM per device.

v0:
```python
import jax
import jax.numpy as jnp
from jax import lax
from jax.sharding import PartitionSpec as P

HD = 128


def sequence_mask(length_row, row_count):
    segment_ends = jnp.cumsum(length_row)
    places = jnp.arange(row_count, dtype=jnp.int32)
    labels = jnp.sum((segment_ends[None, :] <= places[:, None]).astype(jnp.int32), axis=1)
    same = labels[:, None] == labels[None, :]
    return jnp.logical_and(same, places[None, :] <= places[:, None])


def shards(query, keys, values, upstream, projection, lengths):
    row_count, width = query.shape
    head_count = width // HD
    scaling = HD ** (-0.5)
    allowed = sequence_mask(lengths[0], row_count)
    query_heads = query.reshape(row_count, head_count, HD)
    key_heads = keys.reshape(row_count, head_count, HD)
    value_heads = values.reshape(row_count, head_count, HD)
    scores = (
        jnp.einsum("qhd,khd->hqk", query_heads, key_heads, preferred_element_type=jnp.float32)
        * scaling
    )
    scores = jnp.where(allowed[None], scores, -1e30)
    row_max = jnp.max(scores, axis=2, keepdims=True)
    exponent = jnp.exp(scores - row_max)
    probs = exponent / jnp.sum(exponent, axis=2, keepdims=True)
    probs_low = probs.astype(jnp.bfloat16)
    attended = jnp.einsum(
        "hqk,khd->qhd", probs_low, value_heads, preferred_element_type=jnp.float32
    )
    attended = attended.astype(jnp.bfloat16).reshape(row_count, width)
    full_projection = lax.all_gather(projection, "dp", axis=1, tiled=True)
    gathered = lax.all_gather(upstream, "tensor", axis=0, tiled=True)
    out_total = lax.dot_general(
        gathered, full_projection, (((1,), (1,)), ((), ())), preferred_element_type=jnp.float32
    )
    partial_grad = lax.dot_general(
        attended, gathered, (((0,), (0,)), ((), ())), preferred_element_type=jnp.float32
    )
    grad_projection = lax.psum_scatter(
        partial_grad.astype(jnp.bfloat16), "dp", scatter_dimension=1, tiled=True
    ).astype(jnp.float32)
    out_grad = out_total.astype(jnp.bfloat16)
    grad_heads = out_grad.reshape(row_count, head_count, HD)
    grad_values = jnp.einsum(
        "hqk,qhd->khd", probs_low, grad_heads, preferred_element_type=jnp.float32
    ).astype(jnp.bfloat16)
    grad_probs = jnp.einsum(
        "qhd,khd->hqk", grad_heads, value_heads, preferred_element_type=jnp.float32
    )
    delta = jnp.sum(probs * grad_probs, axis=2, keepdims=True)
    grad_scores = (probs * (grad_probs - delta) * scaling).astype(jnp.bfloat16)
    grad_query = jnp.einsum(
        "hqk,khd->qhd", grad_scores, key_heads, preferred_element_type=jnp.float32
    ).astype(jnp.bfloat16)
    grad_keys = jnp.einsum(
        "hqk,qhd->khd", grad_scores, query_heads, preferred_element_type=jnp.float32
    ).astype(jnp.bfloat16)
    return (
        grad_query.reshape(row_count, width),
        grad_keys.reshape(row_count, width),
        grad_values.reshape(row_count, width),
        grad_projection,
    )


def solution(mesh):
    in_specs = (
        P(("groups", "dp"), "tensor"),
        P(("groups", "dp"), "tensor"),
        P(("groups", "dp"), "tensor"),
        P(("groups", "dp", "tensor"), None),
        P("tensor", "dp"),
        P(("groups", "dp"), None),
    )
    out_specs = (
        P(("groups", "dp"), "tensor"),
        P(("groups", "dp"), "tensor"),
        P(("groups", "dp"), "tensor"),
        P(("groups", "tensor"), "dp"),
    )
    return jax.shard_map(shards, mesh=mesh, in_specs=in_specs, out_specs=out_specs, check_vma=False)
```

profile of v0, /device:TPU:0, one launch (start us, length us, event | category | flops | bytes accessed | tf_op | source)
XLA Modules:
  0.0 226.7 jit_solution(17024745603641305551)
XLA Ops:
  7.2 0.0 copy-start
  7.2 0.0 all-gather.3.cloned.1.call-start
  7.2 0.7 all-gather.3.cloned.1.call-update
  7.9 0.0 all-gather.5.cloned.1.call-start
  8.0 0.7 all-gather.5.cloned.1.call-update
  8.7 0.0 reduce-scatter.2.cloned.1.call-start
  8.7 0.8 reduce-window.8
  9.5 0.1 convert_reduce_fusion
  9.6 1.3 fusion.11
  10.9 0.2 fusion.4
  11.1 150.8 %all-gather.3.cloned.1.call-done = bf16[512,8192]{1,0:T(8,128)(2,1)} async-done(((bf16[128,8192]{1,0:T(8,128)(2,1)}), bf16[512,8192]{1,0:T(8,128)(2,1)}) %all-gather.3.cloned.1.call-update) | async-done | bytes 8388624 | tf_op jit(solution)/shard_map/all_gather | solution.py:39
  161.9 0.0 copy-done
  161.9 6.5 %convolution_convert_fusion = bf16[128,8192]{1,0:T(8,128)(2,1)} fusion(bf16[512,8192]{1,0:T(8,128)(2,1)} %all-gather.3.cloned.1.call-done, bf16[512,128]{1,0:T(8,128)(2,1)S(1)} %copy-done, f32[512,512]{0,1:T(8,128)S(1)} %get-tuple-element.13, f32[512]{0:T(512)S(1)} %fusion.4, f32[512]{0:T(512)S(1)} %get-tuple-element.12), kind=kOutput, calls=%fused_computation | convolution fusion | flops 1142751232 | bytes 11669504 | tf_op jit(solution)/shard_map/dot_general | solution.py:43
  168.4 0.0 reduce-scatter.2.cloned.1.call-update
  168.4 15.8 %all-gather.5.cloned.1.call-done = bf16[128,8192]{1,0:T(8,128)(2,1)} async-done(((bf16[128,2048]{1,0:T(8,128)(2,1)}), bf16[128,8192]{1,0:T(8,128)(2,1)}) %all-gather.5.cloned.1.call-update) | async-done | bytes 2097168 | tf_op jit(solution)/shard_map/all_gather | solution.py:38
  184.3 6.3 %convolution_convert_fusion.5 = bf16[512,128]{1,0:T(8,128)(2,1)S(1)} fusion(bf16[512,8192]{1,0:T(8,128)(2,1)} %all-gather.3.cloned.1.call-done, bf16[128,8192]{1,0:T(8,128)(2,1)} %all-gather.5.cloned.1.call-done), kind=kOutput, calls=%fused_computation.7 | convolution fusion | flops 1073807360 | bytes 10616832 | tf_op jit(solution)/shard_map/dot_general | solution.py:40
  190.6 0.3 fusion.1
  190.9 0.0 copy-start.1
  190.9 0.0 copy-start.2
  191.0 0.8 copy.11
  191.7 0.3 multiply_reduce_fusion
  192.0 0.3 multiply_convert_fusion
  192.3 0.0 copy-done.1
  192.3 1.0 convolution_convert_fusion.3
  193.3 0.0 copy-done.2
  193.3 1.0 convolution_convert_fusion.4
  194.3 23.7 %reduce-scatter.2.cloned.1.call-done = bf16[128,2048]{1,0:T(8,128)(2,1)} async-done(((bf16[128,8192]{1,0:T(8,128)(2,1)}), bf16[128,2048]{1,0:T(8,128)(2,1)}) %reduce-scatter.2.cloned.1.call-update) | async-done | bytes 524304 | tf_op jit(solution)/shard_map/reduce_scatter | solution.py:46
  218.0 2.1 convert_element_type.58
Async XLA Ops:
  7.2 154.8 %copy-start = (bf16[512,128]{1,0:T(8,128)(2,1)S(1)}, bf16[512,128]{1,0:T(8,128)(2,1)}, u32[]{:S(2)}) copy-start(bf16[512,128]{1,0:T(8,128)(2,1)} %param.8) | copy-start | bytes 393220
  7.2 154.7 %all-gather.3.cloned.1.call-start = ((), (), s32[]{:S(2)}) async-start(), calls=%async_computation.1 | async-start | bytes 10485760 | tf_op jit(solution)/shard_map/all_gather | solution.py:39
  7.9 176.4 %all-gather.5.cloned.1.call-start = ((), (), s32[]{:S(2)}) async-start(), calls=%async_computation.2 | async-start | bytes 2621440 | tf_op jit(solution)/shard_map/all_gather | solution.py:38
  8.7 209.3 %reduce-scatter.2.cloned.1.call-start = ((), (), s32[]{:S(2)}) async-start(), calls=%async_computation.3 | async-start | bytes 2621440 | tf_op jit(solution)/shard_map/reduce_scatter | solution.py:46
  190.9 1.4 copy-start.1
  190.9 2.4 %copy-start.2 = (bf16[512,128]{1,0:T(8,128)(2,1)S(1)}, bf16[512,128]{1,0:T(8,128)(2,1)}, u32[]{:S(2)}) copy-start(bf16[512,128]{1,0:T(8,128)(2,1)} %param.7) | copy-start | bytes 393220
Sparse Core Ops, SparseCore 0:
  9.6 152.3 all-gather.2
  163.5 20.7 all-gather.4
  186.8 31.1 reduce-scatter.1
where the time goes:
time: 227 us
  waiting for transfers between devices  192 us (85%)
  matrix products  16.7 us (7%)
  between operations  13.8 us (6%)
  other arithmetic  3.53 us (2%)
    all_gather x1, waiting for transfers between devices, shards(): gathered = lax.all_gather(upstream, 'tensor', axis=0, tiled=True)  151 us
    reduce_scatter x1, waiting for transfers between devices, shards(): lax.psum_scatter(partial_grad.astype(jnp.bfloat16), 'dp', scatter_dimensi...  23.7 us
    all_gather x1, waiting for transfers between devices, shards(): full_projection = lax.all_gather(projection, 'dp', axis=1, tiled=True)  15.8 us
    dot_general x1, matrix products, shards(): lax.dot_general(attended, gathered, (((0,), (0,)), ((), ())), preferred_e...  6.48 us
    dot_general x1, matrix products, shards(): lax.dot_general(gathered, full_projection, (((1,), (1,)), ((), ())), pref...  6.31 us
  transfers between devices with their start and end apart: 3, of which 3 were waited for; matrix products, arithmetic and copies ran while one was open for 8% of the time, Pallas kernels for 0%

commit v1 on v0

v1 whole, which is shorter than its diff:
```python
import math

import jax
import jax.numpy as jnp
from jax import lax
from jax.experimental import pallas as pl
from jax.experimental.pallas import tpu as pltpu
from jax.sharding import PartitionSpec as P


HD = 128
CUTS = (0, 2, 3, 4)
TILE = 512


def dot(a, b, contract):
    return lax.dot_general(a, b, ((contract[0], contract[1]), ((), ())), preferred_element_type=jnp.float32)


def build(groups, dp, tensor):
    spans = dp // 2
    bf = jnp.bfloat16
    f32 = jnp.float32
    shared = groups == 2

    def send(value, step, cross):
        perm = [(i, ((i // 2 + step) % spans) * 2 + (i % 2 ^ cross)) for i in range(dp)]
        return lax.ppermute(value, "dp", perm)

    def meet(value, r):
        return lax.ppermute(value, "tensor", [(i, i ^ r) for i in range(tensor)])

    def twin(value):
        return lax.ppermute(value, "groups", [(0, 1), (1, 0)])

    vmem = pl.BlockSpec(memory_space=pltpu.VMEM)
    smem = pl.BlockSpec(memory_space=pltpu.SMEM)
    anywhere = pl.BlockSpec(memory_space=pl.ANY)

    def call(kernel, flops, given, specs, shapes, scratch=(), outs=None, aliases=None):
        moved = sum(x.size * x.dtype.itemsize for x in given if x.size < 1 << 20)
        return pl.pallas_call(
            kernel,
            in_specs=specs,
            out_specs=outs or [vmem] * len(shapes),
            out_shape=[jax.ShapeDtypeStruct(s, t) for s, t in shapes],
            scratch_shapes=list(scratch),
            input_output_aliases=aliases or {},
            cost_estimate=pl.CostEstimate(flops=flops, bytes_accessed=moved, transcendentals=0),
        )(*given)

    def cut_call(upstream, projection, columns, width_of):
        part, given = upstream.shape[0], (upstream,)
        shapes = [(part, w) for w in width_of]
        if projection is not None:
            given += (projection,)
            shapes.append((projection.shape[0] // 2, projection.shape[1]))
        count = len(shapes)

        def kernel(*refs):
            outs, held = refs[len(given) : len(given) + count], refs[len(given) + count : len(given) + 2 * count]
            into, out_of = refs[-2:]
            place = lax.axis_index("dp")
            sources = [refs[0].at[:, pl.ds(pl.multiple_of(f(place), 128), w)] for f, w in zip(columns, width_of)]
            if projection is not None:
                rows = shapes[-1][0]
                sources.append(refs[1].at[pl.ds(pl.multiple_of(lax.axis_index("groups") * rows, rows), rows)])
            loads = [pltpu.make_async_copy(x, held[i], into.at[i]) for i, x in enumerate(sources)]
            stores = [pltpu.make_async_copy(held[i], outs[i], out_of.at[i]) for i in range(count)]
            for load in loads:
                load.start()
            for load, store in zip(loads, stores):
                load.wait()
                store.start()
            for store in stores:
                store.wait()

        return call(
            kernel,
            0,
            given,
            [anywhere] * len(given),
            [(shape, bf) for shape in shapes],
            [pltpu.VMEM(shape, bf) for shape in shapes] + [pltpu.SemaphoreType.DMA((count,))] * 2,
            [anywhere] * count,
        )

    def forward_kernel(lengths_ref, query_ref, keys_ref, values_ref, probs_ref, turned_ref):
        rows = query_ref.shape[0]
        part = turned_ref.shape[2]
        down = lax.broadcasted_iota(jnp.int32, (rows, 1), 0)
        across = lax.broadcasted_iota(jnp.int32, (1, rows), 1)
        label_down, label_across = jnp.zeros_like(down), jnp.zeros_like(across)
        end = jnp.int32(0)
        for c in range(lengths_ref.shape[1]):
            end = end + lengths_ref[0, c]
            label_down += (down >= end).astype(jnp.int32)
            label_across += (across >= end).astype(jnp.int32)
        allowed = jnp.logical_and(label_down == label_across, across <= down)
        scores = dot(query_ref[...], keys_ref[...], ((1,), (1,))) * (HD ** (-0.5))
        scores = jnp.where(allowed, scores, -1e30)
        exponent = jnp.exp(scores - jnp.max(scores, axis=1, keepdims=True))
        probs = exponent / jnp.sum(exponent, axis=1, keepdims=True)
        probs_ref[...] = probs
        if part % 128 == 0:
            turned = dot(values_ref[...], probs.astype(bf), ((0,), (1,))).astype(bf)
            for r in range(tensor):
                turned_ref[r] = turned[:, r * part : (r + 1) * part]
        else:
            attended = dot(probs.astype(bf), values_ref[...], ((1,), (0,)))
            for r in range(tensor):
                turned_ref[r] = jnp.transpose(attended[r * part : (r + 1) * part]).astype(bf)

    def forward_call(lengths, query, keys, values, part):
        rows = query.shape[0]
        return call(
            forward_kernel,
            4 * rows * rows * HD,
            (lengths, query, keys, values),
            [smem] + [vmem] * 3,
            [((rows, rows), f32), ((tensor, HD, part), bf)],
        )

    def backward_kernel(
        probs_ref, query_ref, keys_ref, values_ref, out_grad_ref, grad_query_ref, grad_keys_ref, grad_values_ref
    ):
        out_grad = out_grad_ref[...]
        probs = probs_ref[...]
        grad_probs = dot(out_grad, values_ref[...], ((1,), (1,)))
        delta = jnp.sum(probs * grad_probs, axis=1, keepdims=True)
        grad_scores = (probs * (grad_probs - delta) * (HD ** (-0.5))).astype(bf)
        grad_query_ref[...] = dot(grad_scores, keys_ref[...], ((1,), (0,))).astype(bf)
        grad_keys_ref[...] = dot(grad_scores, query_ref[...], ((0,), (0,))).astype(bf)
        grad_values_ref[...] = dot(probs.astype(bf), out_grad, ((0,), (0,))).astype(bf)

    def whole(shape):
        return pl.BlockSpec(shape, lambda *_: (0, 0))

    def terms_kernel(index_ref, *refs):
        seat = lax.axis_index("tensor")
        blocks = []
        for r in [2 * n for n in range(tensor // 2)] + [2 * n + 1 for n in range(tensor // 2)]:
            at = pl.ds(pl.multiple_of((seat ^ r) * HD, HD), HD)
            blocks.append(jnp.concatenate([a[at, :] for a in refs[:dp]], axis=1))
        attended = jnp.concatenate(blocks, axis=0)
        first, swapped, *rest = refs[dp : 2 * dp]
        held = [first] + rest[: spans - 1] + [swapped] + rest[spans - 1 :]
        held = jnp.concatenate([p[...] for p in held], axis=0)
        kept_ref, low_ref, sent_ref = refs[2 * dp :]
        terms = dot(attended, held, ((1,), (0,)))
        kept_ref[...] = terms[:HD]
        half = tensor // 2 * HD
        if tensor > 2:
            low_ref[...] = terms[HD:half].astype(bf)
        sent_ref[...] = terms[half:].astype(bf)

    def terms_call(place, attended, upstream, swapped, pieces, start):
        part, step = pieces[0].shape
        wide = swapped.shape[1]
        size = math.gcd(math.gcd(step, start), TILE) if start else math.gcd(step, TILE)
        tiles = step // size
        shapes = [((HD, step), f32), ((max(1, tensor // 2 - 1) * HD, step), bf), ((tensor // 2 * HD, step), bf)]
        tile = lambda shape: pl.BlockSpec((shape[0], size), lambda i, *_: (0, i))
        index = jnp.full((1,), (place * wide + start) // size, jnp.int32)
        return pl.pallas_call(
            terms_kernel,
            grid_spec=pltpu.PrefetchScalarGridSpec(
                num_scalar_prefetch=1,
                grid=(tiles,),
                in_specs=[whole(a.shape) for a in attended]
                + [pl.BlockSpec((part, size), lambda i, s: (0, s[0] + i))]
                + [pl.BlockSpec((part, size), lambda i, s: (0, start // size + i))]
                + [tile(p.shape) for p in pieces],
                out_specs=[tile(s) for s, _ in shapes],
            ),
            out_shape=[jax.ShapeDtypeStruct(s, t) for s, t in shapes],
            cost_estimate=pl.CostEstimate(
                flops=2 * dp * part * tensor * HD * step,
                bytes_accessed=2 * (dp * part * tensor * HD + dp * part * step + tensor * HD * step),
                transcendentals=0,
            ),
            name="terms",
        )(index, *attended, upstream, swapped, *pieces)

    def out_kernel(count, index_ref, upstream_ref, swapped_ref, base_ref, *refs):
        many = (tensor - 1) * (2 if shared else 1)
        blocks, pieces, (kept_ref, sent_ref, full) = refs[:many], refs[many:-3], refs[-3:]
        part = upstream_ref.shape[0]
        seat = lax.axis_index("tensor")
        full[pl.ds(pl.multiple_of(seat * HD, HD), HD)] = base_ref[...]
        for r in range(1, tensor):
            at = (seat ^ r) * HD
            if shared:
                half = HD // 2
                mine = lax.axis_index("groups") * half
                full[pl.ds(pl.multiple_of(at + mine, half), half)] = blocks[2 * r - 2][...]
                full[pl.ds(pl.multiple_of(at + half - mine, half), half)] = blocks[2 * r - 1][...]
            else:
                full[pl.ds(pl.multiple_of(at, HD), HD)] = blocks[r - 1][...]
        rows = [jnp.concatenate([pieces[c * (dp - 2) + p][...] for c in range(count)], axis=1) for p in range(dp - 2)]
        rows = [upstream_ref[...]] + rows[: spans - 1] + [swapped_ref[...]] + rows[spans - 1 :]
        total = dot(jnp.concatenate(rows, axis=0), full[...], ((1,), (1,)))
        half = spans * part
        kept_ref[...] = total[:half]
        sent_ref[...] = total[half:].astype(bf)

    def out_call(index, upstream, swapped, projection, blocks, pieces):
        part, wide, count = upstream.shape[0], projection.shape[1], len(pieces)
        flat = [p for row in pieces for p in row]
        shape = (spans * part, tensor * HD)
        return pl.pallas_call(
            lambda *refs: out_kernel(count, *refs),
            grid_spec=pltpu.PrefetchScalarGridSpec(
                num_scalar_prefetch=1,
                grid=(1,),
                in_specs=[pl.BlockSpec((part, wide), lambda i, s: (0, s[0]))]
                + [whole(p.shape) for p in [swapped, projection] + blocks + flat],
                out_specs=[whole(shape)] * 2,
                scratch_shapes=[pltpu.VMEM((tensor * HD, wide), bf)],
            ),
            out_shape=[jax.ShapeDtypeStruct(shape, f32), jax.ShapeDtypeStruct(shape, bf)],
            cost_estimate=pl.CostEstimate(
                flops=4 * shape[0] * shape[1] * wide,
                bytes_accessed=2 * (dp * part * wide + tensor * projection.size + 3 * shape[0] * shape[1]),
                transcendentals=0,
            ),
            name="outs",
        )(index, upstream, swapped, projection, *blocks, *flat)

    def shards(query, keys, values, upstream, projection, lengths):
        rows = query.shape[0]
        part = upstream.shape[0]
        wide = projection.shape[1]
        place = lax.axis_index("dp")
        bounds = [wide * cut // CUTS[-1] for cut in CUTS]
        chunks = list(zip(bounds, bounds[1:]))
        ways = [(j, 0) for j in range(1, spans)] + [(j, 1) for j in range(1, spans)]

        def cut(source, parts, extra, swap):
            columns, widths = [], []
            for c in parts:
                for j, cross in ways:
                    start, stop = chunks[c]
                    columns.append(lambda p, j=j, cross=cross, start=start: target(p, j, cross) * wide + start)
                    widths.append(stop - start)
            if swap:
                columns.append(lambda p: target(p, 0, 1) * wide)
                widths.append(wide)
            return cut_call(source, extra, columns, widths)

        def target(p, j, cross):
            return ((p // 2 + j) % spans) * 2 + ((p % 2) ^ cross)

        def spread(pieces):
            return [send(x, j, cross) for x, (j, cross) in zip(pieces, ways)]

        first = cut(upstream, [0], projection if shared else None, False)
        held = [spread(first)]

        probs, turned = forward_call(lengths, query, keys, values, part)
        mine = lax.all_to_all(turned, "tensor", 0, 0, tiled=True).reshape(tensor * HD, part)
        over = [mine] + [send(mine, j, 0) for j in range(1, spans)]
        attended = over + [send(piece, 0, 1) for piece in over]

        later, _ = lax.optimization_barrier((upstream, turned))
        rest = cut(later, range(1, len(chunks)), None, True)
        for c in range(1, len(chunks)):
            held.append(spread(rest[(c - 1) * len(ways) :]))
        swapped = send(rest[-1], 0, 1)

        half = first[-1] if shared else projection
        known = {0: half}
        bit = tensor // 2
        while bit:
            known.update({r ^ bit: meet(block, bit) for r, block in sorted(known.items())})
            bit //= 2
        blocks = []
        for r in range(1, tensor):
            blocks += [known[r], twin(known[r])] if shared else [known[r]]

        grad_projection = None
        for c, (start, stop) in enumerate(chunks):
            step = stop - start
            kept, low, sent = terms_call(place, attended, upstream, swapped, held[c], start)
            near = meet(sent, 1)
            rest = []
            for n in range(1, tensor // 2):
                rest.append(low[(n - 1) * HD : n * HD] + near[n * HD : (n + 1) * HD])
            rest = dict(enumerate(rest, 1))
            far, bit = [], 1
            while rest:
                going = [n for n in sorted(rest) if n & bit]
                bundle = rest[going[0]] if len(going) == 1 else jnp.concatenate([rest[n] for n in going], axis=0)
                came = meet(bundle, 2 * bit)
                rest = {n: v for n, v in rest.items() if not n & bit}
                for i, n in enumerate(going):
                    piece = came[i * HD : (i + 1) * HD] if len(going) > 1 else came
                    if n == bit:
                        far.append(piece)
                    else:
                        rest[n ^ bit] = rest[n ^ bit] + piece
                bit *= 2
            total = kept + near[:HD].astype(f32)
            for piece in far:
                total = total + piece.astype(f32)
            if grad_projection is None:
                grad_projection = jnp.pad(total, ((0, 0), (0, wide - step)))
            else:
                grad_projection = lax.dynamic_update_slice(grad_projection, total, (0, start))

        kept, sent = out_call(jnp.full((1,), place, jnp.int32), upstream, swapped, projection, blocks, held)
        summed = kept + send(sent, 0, 1).astype(f32)
        own_rows = summed[:part]
        for j in range(1, spans):
            own_rows = own_rows + send(summed[j * part : (j + 1) * part].astype(bf), -j, 0).astype(f32)
        own_rows = own_rows.astype(bf)
        pieces = jnp.transpose(own_rows.reshape(part, tensor, HD), (1, 0, 2))
        out_grad = lax.all_to_all(pieces, "tensor", 0, 0, tiled=True).reshape(rows, HD)

        grads = call(
            backward_kernel,
            10 * rows * rows * HD,
            (probs, query, keys, values, out_grad),
            [vmem] * 5,
            [((rows, HD), bf)] * 3,
        )
        return (*grads, grad_projection)

    return shards


def solution(mesh):
    in_specs = (
        P(("groups", "dp"), "tensor"),
        P(("groups", "dp"), "tensor"),
        P(("groups", "dp"), "tensor"),
        P(("groups", "dp", "tensor"), None),
        P("tensor", "dp"),
        P(("groups", "dp"), None),
    )
    out_specs = (
        P(("groups", "dp"), "tensor"),
        P(("groups", "dp"), "tensor"),
        P(("groups", "dp"), "tensor"),
        P(("groups", "tensor"), "dp"),
    )
    shards = build(mesh.shape["groups"], mesh.shape["dp"], mesh.shape["tensor"])

    return jax.shard_map(shards, mesh=mesh, in_specs=in_specs, out_specs=out_specs, check_vma=False)
```

time: 227 us -> 100 us (0.44)
  waiting for transfers between devices: 192 us -> 36.5 us
  starting transfers between devices: 0.11 us -> 35.6 us
  Pallas kernels: 0 us -> 22.4 us
  matrix products: 16.7 us -> 0 us
  between operations: 13.8 us -> 0.93 us
    all_gather x2 -> x0, waiting for transfers between devices: 167 us -> none  [the longest x1 151 us: shards(): gathered = lax.all_gather(upstream, 'tensor', axis=0, tiled=True)]
    ppermute x0 -> x24, waiting for transfers between devices: none -> 31.3 us  [the longest x9 19.1 us: meet(): return lax.ppermute(value, 'tensor', [(i, i ^ r) for i in range(tensor)])]
    ppermute x0 -> x24, starting transfers between devices: none -> 28.5 us  [the longest x9 14.9 us: meet(): return lax.ppermute(value, 'tensor', [(i, i ^ r) for i in range(tensor)])]
    reduce_scatter x1 -> x0, waiting for transfers between devices: 23.7 us -> none  [shards(): lax.psum_scatter(partial_grad.astype(jnp.bfloat16), 'dp', scatter_dimensi...]
    pallas_call x0 -> x8, Pallas kernels: none -> 22.4 us  [the longest x4 9.88 us: call(): pl.pallas_call(kernel, in_specs=specs, out_specs=outs or [vmem] * len(sha...]
    dot_general x7 -> x0, matrix products: 16.7 us -> none  [the longest x1 6.48 us: shards(): lax.dot_general(attended, gathered, (((0,), (0,)), ((), ())), preferred_e...]
    all_to_all x0 -> x2, starting transfers between devices: none -> 7.1 us  [the longest x1 3.78 us: shards(): lax.all_to_all(pieces, 'tensor', 0, 0, tiled=True).reshape(rows, HD)]
    all_to_all x0 -> x2, waiting for transfers between devices: none -> 5.19 us  [the longest x1 4.55 us: shards(): lax.all_to_all(turned, 'tensor', 0, 0, tiled=True)]
  transfers between devices with their start and end apart: 3 -> 26, of which waited for: 3 -> 12; matrix products, arithmetic and copies ran while one was open for 8% -> 3% of each run, Pallas kernels for 0% -> 14%
where the time goes in v1:
time: 100 us; the launch traced here: 99.7 us
  waiting for transfers between devices  36.5 us (36%)
  starting transfers between devices  35.6 us (36%)
  Pallas kernels  22.4 us (22%)
  other arithmetic  2.81 us (3%)
  local copies, waits for them, and re-layouts  1.55 us (2%)
    ppermute x9, waiting for transfers between devices, meet(): return lax.ppermute(value, 'tensor', [(i, i ^ r) for i in range(tensor)])  19.1 us
    ppermute x9, starting transfers between devices, meet(): return lax.ppermute(value, 'tensor', [(i, i ^ r) for i in range(tensor)])  14.9 us
    ppermute x12, starting transfers between devices, send(): return lax.ppermute(value, 'dp', perm)  10 us
    pallas_call x4, Pallas kernels, call(): pl.pallas_call(kernel, in_specs=specs, out_specs=outs or [vmem] * len(sha...  9.88 us
    pallas_call x3, Pallas kernels, terms_call(): pl.pallas_call(terms_kernel, grid_spec=pltpu.PrefetchScalarGridSpec(num_s...  8.11 us
    ppermute x12, waiting for transfers between devices, send(): return lax.ppermute(value, 'dp', perm)  7.29 us
    ppermute x3, waiting for transfers between devices, twin(): return lax.ppermute(value, 'groups', [(0, 1), (1, 0)])  4.9 us
    all_to_all x1, waiting for transfers between devices, shards(): lax.all_to_all(turned, 'tensor', 0, 0, tiled=True)  4.55 us
  transfers between devices with their start and end apart: 26, of which 12 were waited for; matrix products, arithmetic and copies ran while one was open for 3% of the time, Pallas kernels for 14%

profile of v1, /device:TPU:0, one launch (start us, length us, event | category | flops | bytes accessed | tf_op | source)
XLA Modules:
  0.0 99.7 jit_solution(1887862669530190666)
XLA Ops:
  0.6 2.7 %shard_map.93 = (f32[512,512]{1,0:T(8,128)}, bf16[4,128,128]{2,1,0:T(8,128)(2,1)}) custom-call(s32[1,8]{1,0:T(1,128)} %lengths_ref.1, bf16[512,128]{1,0:T(8,128)(2,1)} %query_ref.3, bf16[512,128]{1,0:T(8,128)(2,1)} %keys_ref.3, bf16[512,128]{1,0:T(8,128)(2,1)} %values_ref.3), custom_call_target="tpu_custom_call" | custom-call | flops 134217728 | bytes 393248 | tf_op jit(solution)/shard_map/pallas_call | solution.py:42
  3.3 2.2 %shard_map.94 = (bf16[128,512]{1,0:T(8,128)(2,1)}, bf16[128,512]{1,0:T(8,128)(2,1)}, bf16[128,512]{1,0:T(8,128)(2,1)}, bf16[128,512]{1,0:T(8,128)(2,1)}, bf16[128,2048]{1,0:T(8,128)(2,1)}) custom-call(bf16[128,8192]{1,0:T(8,128)(2,1)} %refs_4_.5), custom_call_target="tpu_custom_call" | custom-call | tf_op jit(solution)/shard_map/pallas_call | solution.py:42
  5.6 3.0 %collective-permute-start.9 = (bf16[128,512]{1,0:T(8,128)(2,1)}, bf16[128,512]{1,0:T(8,128)(2,1)S(1)}, u32[]{:S(2)}, u32[]{:S(2)}) collective-permute-start(bf16[128,512]{1,0:T(8,128)(2,1)} %get-tuple-element.36), channel_id=1, source_target_pairs={{0,8},{4,12},{8,0},{12,4},{1,9},{5,13},{9,1},{13,5},{2,10},{6,14},... | collective-permute-start | bytes 393224 | tf_op jit(solution)/shard_map/ppermute | solution.py:28
  8.6 1.9 %shard_map.95 = (bf16[128,1024]{1,0:T(8,128)(2,1)}, bf16[128,1024]{1,0:T(8,128)(2,1)}, bf16[64,2048]{1,0:T(8,128)(2,1)}) custom-call(bf16[128,8192]{1,0:T(8,128)(2,1)} %refs_4_.5, bf16[128,2048]{1,0:T(8,128)(2,1)} %refs_3_.1), custom_call_target="tpu_custom_call" | custom-call | bytes 524288 | tf_op jit(solution)/shard_map/pallas_call | solution.py:42
  10.5 2.7 %collective-permute-start.3 = (bf16[64,2048]{1,0:T(8,128)(2,1)}, bf16[64,2048]{1,0:T(8,128)(2,1)S(1)}, u32[]{:S(2)}, u32[]{:S(2)}) collective-permute-start(bf16[64,2048]{1,0:T(8,128)(2,1)} %get-tuple-element.33), channel_id=1, source_target_pairs={{0,2},{1,3},{2,0},{3,1},{4,6},{5,7},{6,4},{7,5},{8,10},{9,11},{10,... | collective-permute-start | bytes 786440 | tf_op jit(solution)/shard_map/ppermute | solution.py:31
  13.1 3.3 %all-to-all-start.1 = ((bf16[4,128,128]{2,1,0:T(8,128)(2,1)}), bf16[4,128,128]{2,1,0:T(8,128)(2,1)S(1)}, u32[]{:S(2)}, u32[]{:S(2)}) async-start(bf16[4,128,128]{2,1,0:T(8,128)(2,1)} %get-tuple-element.30), calls=%async_computation.1 | async-start | bytes 262144 | tf_op jit(solution)/shard_map/all_to_all | solution.py:261
  16.5 2.0 %collective-permute-start.1 = (bf16[64,2048]{1,0:T(8,128)(2,1)}, bf16[64,2048]{1,0:T(8,128)(2,1)S(1)}, u32[]{:S(2)}, u32[]{:S(2)}) collective-permute-start(bf16[64,2048]{1,0:T(8,128)(2,1)} %get-tuple-element.33), channel_id=1, source_target_pairs={{0,1},{1,0},{2,3},{3,2},{4,5},{5,4},{6,7},{7,6},{8,9},{9,8},{10,11... | collective-permute-start | bytes 786440 | tf_op jit(solution)/shard_map/ppermute | solution.py:31
  18.5 1.3 %collective-permute-start.11 = (bf16[128,512]{1,0:T(8,128)(2,1)S(1)}, bf16[128,512]{1,0:T(8,128)(2,1)S(1)}, u32[]{:S(2)}, u32[]{:S(2)}) collective-permute-start(bf16[128,512]{1,0:T(8,128)(2,1)S(1)} %copy-done.26), channel_id=1, source_target_pairs={{0,8},{4,12},{8,0},{12,4},{1,9},{5,13},{9,1},{13,5},{2,10},{6,14},... | collective-permute-start | bytes 393224 | tf_op jit(solution)/shard_map/ppermute | solution.py:28
  19.8 4.4 %collective-permute-done.10.refs_13_.refs_7_ = bf16[128,512]{1,0:T(8,128)(2,1)S(1)} collective-permute-done((bf16[128,512]{1,0:T(8,128)(2,1)S(1)}, bf16[128,512]{1,0:T(8,128)(2,1)S(1)}, u32[]{:S(2)}, u32[]{:S(2)}) %collective-permute-start.10) | collective-permute-done | bytes 131104 | tf_op jit(solution)/shard_map/ppermute | solution.py:28
  24.3 4.5 %all-to-all-done.1 = bf16[4,128,128]{2,1,0:T(8,128)(2,1)S(1)} async-done(((bf16[4,128,128]{2,1,0:T(8,128)(2,1)}), bf16[4,128,128]{2,1,0:T(8,128)(2,1)S(1)}, u32[]{:S(2)}, u32[]{:S(2)}) %all-to-all-start.1) | async-done | bytes 131104 | tf_op jit(solution)/shard_map/all_to_all | solution.py:261
  28.8 0.5 collective-permute-start.15
  29.3 0.9 collective-permute-start.5
  30.2 1.5 %collective-permute-done.1.refs_4_ = bf16[64,2048]{1,0:T(8,128)(2,1)S(1)} collective-permute-done((bf16[64,2048]{1,0:T(8,128)(2,1)}, bf16[64,2048]{1,0:T(8,128)(2,1)S(1)}, u32[]{:S(2)}, u32[]{:S(2)}) %collective-permute-start.1) | collective-permute-done | bytes 262176 | tf_op jit(solution)/shard_map/ppermute | solution.py:31
  31.7 0.5 collective-permute-start.7
  32.2 1.6 %collective-permute-done.15.refs_1_ = bf16[512,128]{1,0:T(8,128)(2,1)S(1)} collective-permute-done((bf16[512,128]{1,0:T(8,128)(2,1)S(1)}, bf16[512,128]{1,0:T(8,128)(2,1)S(1)}, u32[]{:S(2)}, u32[]{:S(2)}) %collective-permute-start.15) | collective-permute-done | bytes 131104 | tf_op jit(solution)/shard_map/ppermute | solution.py:28
  33.8 0.9 collective-permute-start.17
  34.8 1.0 collective-permute-done.17.refs_3_
  35.7 1.2 %collective-permute-start.4 = (bf16[64,2048]{1,0:T(8,128)(2,1)S(1)}, bf16[64,2048]{1,0:T(8,128)(2,1)S(1)}, u32[]{:S(2)}, u32[]{:S(2)}) collective-permute-start(bf16[64,2048]{1,0:T(8,128)(2,1)S(1)} %collective-permute-done.3.refs_6_), channel_id=1, source_target_pairs={{0,16},{16,0},{1,17},{17,1},{2,18},{18,2},{3,19},{19,3},{4,20},{20... | collective-permute-start | bytes 786440 | tf_op jit(solution)/shard_map/ppermute | solution.py:34
  37.0 0.8 collective-permute-start.2
  37.8 0.3 collective-permute-done.5.refs_8_
  38.0 1.6 %collective-permute-start.6 = (bf16[64,2048]{1,0:T(8,128)(2,1)S(1)}, bf16[64,2048]{1,0:T(8,128)(2,1)S(1)}, u32[]{:S(2)}, u32[]{:S(2)}) collective-permute-start(bf16[64,2048]{1,0:T(8,128)(2,1)S(1)} %collective-permute-done.5.refs_8_), channel_id=1, source_target_pairs={{0,16},{16,0},{1,17},{17,1},{2,18},{18,2},{3,19},{19,3},{4,20},{20... | collective-permute-start | bytes 786440 | tf_op jit(solution)/shard_map/ppermute | solution.py:34
  39.6 2.5 %terms.4 = (f32[128,512]{1,0:T(8,128)}, bf16[128,512]{1,0:T(8,128)(2,1)}, bf16[256,512]{1,0:T(8,128)(2,1)}) custom-call(s32[1]{0:T(128)} %bitcast.5.index_ref, bf16[512,128]{1,0:T(8,128)(2,1)} %bitcast.15, bf16[512,128]{1,0:T(8,128)(2,1)} %copy-done.2, bf16[512,128]{1,0:T(8,128)(2,1)} %copy-done.3, bf16[512,128]{1,0:T(8,128)(2,1)} %copy-done.4, ...), custom_call_target="tpu_custom_call" | custom-call | flops 268435456 | bytes 1572864 | tf_op jit(solution)/shard_map/terms/pallas_call | solution.py:165
  42.1 1.2 %collective-permute-start.20 = (bf16[256,512]{1,0:T(8,128)(2,1)}, bf16[256,512]{1,0:T(8,128)(2,1)}, u32[]{:S(2)}, u32[]{:S(2)}) collective-permute-start(bf16[256,512]{1,0:T(8,128)(2,1)} %get-tuple-element.49), channel_id=1, source_target_pairs={{0,1},{1,0},{2,3},{3,2},{4,5},{5,4},{6,7},{7,6},{8,9},{9,8},{10,11... | collective-permute-start | bytes 786440 | tf_op jit(solution)/shard_map/ppermute | solution.py:31
  43.3 0.2 collective-permute-done.8.refs_11_.refs_7_
  43.5 2.1 %collective-permute-start.12 = (bf16[128,512]{1,0:T(8,128)(2,1)}, bf16[128,512]{1,0:T(8,128)(2,1)S(1)}, u32[]{:S(2)}, u32[]{:S(2)}) collective-permute-start(bf16[128,512]{1,0:T(8,128)(2,1)} %get-tuple-element.39), channel_id=1, source_target_pairs={{0,12},{4,8},{8,4},{12,0},{1,13},{5,9},{9,5},{13,1},{2,14},{6,10},... | collective-permute-start | bytes 393224 | tf_op jit(solution)/shard_map/ppermute | solution.py:28
  45.6 3.1 %terms.3 = (f32[128,1024]{1,0:T(8,128)}, bf16[128,1024]{1,0:T(8,128)(2,1)}, bf16[256,1024]{1,0:T(8,128)(2,1)}) custom-call(s32[1]{0:T(128)} %bitcast.3.index_ref, bf16[512,128]{1,0:T(8,128)(2,1)} %bitcast.16, bf16[512,128]{1,0:T(8,128)(2,1)} %copy-done.2, bf16[512,128]{1,0:T(8,128)(2,1)} %copy-done.3, bf16[512,128]{1,0:T(8,128)(2,1)} %copy-done.4, ...), custom_call_target="tpu_custom_call" | custom-call | flops 536870912 | bytes 2621440 | tf_op jit(solution)/shard_map/terms/pallas_call | solution.py:165
  48.7 1.9 %collective-permute-start.18 = (bf16[256,1024]{1,0:T(8,128)(2,1)}, bf16[256,1024]{1,0:T(8,128)(2,1)S(1)}, u32[]{:S(2)}, u32[]{:S(2)}) collective-permute-start(bf16[256,1024]{1,0:T(8,128)(2,1)} %get-tuple-element.46), channel_id=1, source_target_pairs={{0,1},{1,0},{2,3},{3,2},{4,5},{5,4},{6,7},{7,6},{8,9},{9,8},{10,11... | collective-permute-start | bytes 1572872 | tf_op jit(solution)/shard_map/ppermute | solution.py:31
  50.7 4.9 %collective-permute-done.6.refs_9_ = bf16[64,2048]{1,0:T(8,128)(2,1)S(1)} collective-permute-done((bf16[64,2048]{1,0:T(8,128)(2,1)S(1)}, bf16[64,2048]{1,0:T(8,128)(2,1)S(1)}, u32[]{:S(2)}, u32[]{:S(2)}) %collective-permute-start.6) | collective-permute-done | bytes 262176 | tf_op jit(solution)/shard_map/ppermute | solution.py:34
  55.6 0.7 copy-done.21
  56.3 4.4 %outs.1 = (f32[256,512]{1,0:T(8,128)}, bf16[256,512]{1,0:T(8,128)(2,1)}) custom-call(s32[1]{0:T(128)} %bitcast.refs_0_, bf16[128,8192]{1,0:T(8,128)(2,1)} %refs_4_.5, bf16[128,2048]{1,0:T(8,128)(2,1)} %copy-done, bf16[128,2048]{1,0:T(8,128)(2,1)} %refs_3_.1, bf16[64,2048]{1,0:T(8,128)(2,1)} %copy-done.17, bf16[64,2048]{1,0:T(8,128)(2,1)} %copy-done.20, ...), custom_call_target="tpu_custom_call" | custom-call | flops 1073741824 | bytes 4980736 | tf_op jit(solution)/shard_map/outs/pallas_call | solution.py:211
  60.8 2.5 %terms.5 = (f32[128,512]{1,0:T(8,128)}, bf16[128,512]{1,0:T(8,128)(2,1)}, bf16[256,512]{1,0:T(8,128)(2,1)}) custom-call(s32[1]{0:T(128)} %bitcast.6.index_ref, bf16[512,128]{1,0:T(8,128)(2,1)} %bitcast.17, bf16[512,128]{1,0:T(8,128)(2,1)} %copy-done.2, bf16[512,128]{1,0:T(8,128)(2,1)} %copy-done.3, bf16[512,128]{1,0:T(8,128)(2,1)} %copy-done.4, ...), custom_call_target="tpu_custom_call" | custom-call | flops 268435456 | bytes 1572864 | tf_op jit(solution)/shard_map/terms/pallas_call | solution.py:165
  63.3 1.3 %collective-permute-start.22 = (bf16[256,512]{1,0:T(8,128)(2,1)}, bf16[256,512]{1,0:T(8,128)(2,1)S(1)}, u32[]{:S(2)}, u32[]{:S(2)}) collective-permute-start(bf16[256,512]{1,0:T(8,128)(2,1)} %get-tuple-element.52), channel_id=1, source_target_pairs={{0,1},{1,0},{2,3},{3,2},{4,5},{5,4},{6,7},{7,6},{8,9},{9,8},{10,11... | collective-permute-start | bytes 786440 | tf_op jit(solution)/shard_map/ppermute | solution.py:31
  64.6 0.9 slice_add_fusion.3
  65.5 3.2 %collective-permute-start.21 = (bf16[128,512]{1,0:T(8,128)(2,1)S(1)}, bf16[128,512]{1,0:T(8,128)(2,1)S(1)}, u32[]{:S(2)}, u32[]{:S(2)}) collective-permute-start(bf16[128,512]{1,0:T(8,128)(2,1)S(1)} %slice_add_fusion.3), channel_id=1, source_target_pairs={{0,2},{1,3},{2,0},{3,1},{4,6},{5,7},{6,4},{7,5},{8,10},{9,11},{10,... | collective-permute-start | bytes 393224 | tf_op jit(solution)/shard_map/ppermute | solution.py:31
  68.8 1.6 %collective-permute-start.14 = (bf16[128,512]{1,0:T(8,128)(2,1)S(1)}, bf16[128,512]{1,0:T(8,128)(2,1)S(1)}, u32[]{:S(2)}, u32[]{:S(2)}) collective-permute-start(bf16[128,512]{1,0:T(8,128)(2,1)S(1)} %slice.53), channel_id=1, source_target_pairs={{0,8},{4,12},{8,0},{12,4},{1,9},{5,13},{9,1},{13,5},{2,10},{6,14},... | collective-permute-start | bytes 393224 | tf_op jit(solution)/shard_map/ppermute | solution.py:28
  70.3 0.3 collective-permute-start.19
  70.7 5.1 %collective-permute-done.22 = bf16[256,512]{1,0:T(8,128)(2,1)S(1)} collective-permute-done((bf16[256,512]{1,0:T(8,128)(2,1)}, bf16[256,512]{1,0:T(8,128)(2,1)S(1)}, u32[]{:S(2)}, u32[]{:S(2)}) %collective-permute-start.22) | collective-permute-done | bytes 262176 | tf_op jit(solution)/shard_map/ppermute | solution.py:31
  75.8 1.6 %collective-permute-start.23 = (bf16[128,512]{1,0:T(8,128)(2,1)S(1)}, bf16[128,512]{1,0:T(8,128)(2,1)S(1)}, u32[]{:S(2)}, u32[]{:S(2)}) collective-permute-start(bf16[128,512]{1,0:T(8,128)(2,1)S(1)} %slice_add_fusion.2), channel_id=1, source_target_pairs={{0,2},{1,3},{2,0},{3,1},{4,6},{5,7},{6,4},{7,5},{8,10},{9,11},{10,... | collective-permute-start | bytes 393224 | tf_op jit(solution)/shard_map/ppermute | solution.py:31
  77.4 0.7 bitcast_bitcast_fusion
  78.1 3.8 %all-to-all-start = ((bf16[4,128,128]{2,1,0:T(8,128)(2,1)}), bf16[4,128,128]{2,1,0:T(8,128)(2,1)S(1)}, u32[]{:S(2)}, u32[]{:S(2)}) async-start(bf16[4,128,128]{2,1,0:T(8,128)(2,1)} %bitcast_bitcast_fusion), calls=%async_computation | async-start | bytes 262144 | tf_op jit(solution)/shard_map/all_to_all | solution.py:318
  81.9 10.7 %collective-permute-done.19 = bf16[128,1024]{1,0:T(8,128)(2,1)S(1)} collective-permute-done((bf16[128,1024]{1,0:T(8,128)(2,1)S(1)}, bf16[128,1024]{1,0:T(8,128)(2,1)S(1)}, u32[]{:S(2)}, u32[]{:S(2)}) %collective-permute-start.19) | collective-permute-done | bytes 262176 | tf_op jit(solution)/shard_map/ppermute | solution.py:31
  92.6 0.1 convert_add_fusion
  92.7 0.1 pad.4
  92.8 0.9 add_dynamic-update-slice_fusion.1
  93.7 1.5 %collective-permute-done.23 = bf16[128,512]{1,0:T(8,128)(2,1)S(1)} collective-permute-done((bf16[128,512]{1,0:T(8,128)(2,1)S(1)}, bf16[128,512]{1,0:T(8,128)(2,1)S(1)}, u32[]{:S(2)}, u32[]{:S(2)}) %collective-permute-start.23) | collective-permute-done | bytes 131104 | tf_op jit(solution)/shard_map/ppermute | solution.py:31
  95.3 0.6 all-to-all-done
  96.0 0.7 copy-done.13
  96.6 3.1 %shard_map.96 = (bf16[512,128]{1,0:T(8,128)(2,1)}, bf16[512,128]{1,0:T(8,128)(2,1)}, bf16[512,128]{1,0:T(8,128)(2,1)}) custom-call(f32[512,512]{1,0:T(8,128)} %get-tuple-element.29.probs_ref, bf16[512,128]{1,0:T(8,128)(2,1)} %query_ref.3, bf16[512,128]{1,0:T(8,128)(2,1)} %keys_ref.3, bf16[512,128]{1,0:T(8,128)(2,1)} %values_ref.3, bf16[512,128]{1,0:T(8,128)(2,1)} %bitcast.18), custom_call_target="tpu_custom_call" | custom-call | flops 335544320 | bytes 1572864 | tf_op jit(solution)/shard_map/pallas_call | solution.py:42
  (78 shorter events, 0.4 us)
Async XLA Ops:
  5.5 12.9 %copy-start.27 = (bf16[128,512]{1,0:T(8,128)(2,1)S(1)}, bf16[128,512]{1,0:T(8,128)(2,1)}, u32[]{:S(2)}) copy-start(bf16[128,512]{1,0:T(8,128)(2,1)} %get-tuple-element.37) | copy-start | bytes 393220
  5.5 12.9 %copy-start.26 = (bf16[128,512]{1,0:T(8,128)(2,1)S(1)}, bf16[128,512]{1,0:T(8,128)(2,1)}, u32[]{:S(2)}) copy-start(bf16[128,512]{1,0:T(8,128)(2,1)} %get-tuple-element.38) | copy-start | bytes 393220
  5.6 12.9 %collective-permute-start.9 = (bf16[128,512]{1,0:T(8,128)(2,1)}, bf16[128,512]{1,0:T(8,128)(2,1)S(1)}, u32[]{:S(2)}, u32[]{:S(2)}) collective-permute-start(bf16[128,512]{1,0:T(8,128)(2,1)} %get-tuple-element.36), channel_id=1, source_target_pairs={{0,8},{4,12},{8,0},{12,4},{1,9},{5,13},{9,1},{13,5},{2,10},{6,14},... | collective-permute-start | bytes 393224 | tf_op jit(solution)/shard_map/ppermute | solution.py:28
  8.6 28.4 %collective-permute-start = (bf16[128,2048]{1,0:T(8,128)(2,1)}, bf16[128,2048]{1,0:T(8,128)(2,1)S(1)}, u32[]{:S(2)}, u32[]{:S(2)}) collective-permute-start(bf16[128,2048]{1,0:T(8,128)(2,1)} %get-tuple-element.32), channel_id=1, source_target_pairs={{0,4},{4,0},{8,12},{12,8},{1,5},{5,1},{9,13},{13,9},{2,6},{6,2},{1... | collective-permute-start | bytes 1572872 | tf_op jit(solution)/shard_map/ppermute | solution.py:28
  10.5 18.8 %collective-permute-start.3 = (bf16[64,2048]{1,0:T(8,128)(2,1)}, bf16[64,2048]{1,0:T(8,128)(2,1)S(1)}, u32[]{:S(2)}, u32[]{:S(2)}) collective-permute-start(bf16[64,2048]{1,0:T(8,128)(2,1)} %get-tuple-element.33), channel_id=1, source_target_pairs={{0,2},{1,3},{2,0},{3,1},{4,6},{5,7},{6,4},{7,5},{8,10},{9,11},{10,... | collective-permute-start | bytes 786440 | tf_op jit(solution)/shard_map/ppermute | solution.py:31
  13.1 15.7 %all-to-all-start.1 = ((bf16[4,128,128]{2,1,0:T(8,128)(2,1)}), bf16[4,128,128]{2,1,0:T(8,128)(2,1)S(1)}, u32[]{:S(2)}, u32[]{:S(2)}) async-start(bf16[4,128,128]{2,1,0:T(8,128)(2,1)} %get-tuple-element.30), calls=%async_computation.1 | async-start | bytes 262144 | tf_op jit(solution)/shard_map/all_to_all | solution.py:261
  16.5 15.2 %collective-permute-start.1 = (bf16[64,2048]{1,0:T(8,128)(2,1)}, bf16[64,2048]{1,0:T(8,128)(2,1)S(1)}, u32[]{:S(2)}, u32[]{:S(2)}) collective-permute-start(bf16[64,2048]{1,0:T(8,128)(2,1)} %get-tuple-element.33), channel_id=1, source_target_pairs={{0,1},{1,0},{2,3},{3,2},{4,5},{5,4},{6,7},{7,6},{8,9},{9,8},{10,11... | collective-permute-start | bytes 786440 | tf_op jit(solution)/shard_map/ppermute | solution.py:31
  18.5 5.8 %collective-permute-start.10 = (bf16[128,512]{1,0:T(8,128)(2,1)S(1)}, bf16[128,512]{1,0:T(8,128)(2,1)S(1)}, u32[]{:S(2)}, u32[]{:S(2)}) collective-permute-start(bf16[128,512]{1,0:T(8,128)(2,1)S(1)} %copy-done.27), channel_id=1, source_target_pairs={{0,12},{4,8},{8,4},{12,0},{1,13},{5,9},{9,5},{13,1},{2,14},{6,10},... | collective-permute-start | bytes 393224 | tf_op jit(solution)/shard_map/ppermute | solution.py:28
  18.5 21.1 %copy-start.10 = (bf16[128,512]{1,0:T(8,128)(2,1)}, bf16[128,512]{1,0:T(8,128)(2,1)S(1)}, u32[]{:S(2)}) copy-start(bf16[128,512]{1,0:T(8,128)(2,1)S(1)} %collective-permute-done.9.refs_12_.refs_6_) | copy-start | bytes 393220
  18.5 10.8 %collective-permute-start.11 = (bf16[128,512]{1,0:T(8,128)(2,1)S(1)}, bf16[128,512]{1,0:T(8,128)(2,1)S(1)}, u32[]{:S(2)}, u32[]{:S(2)}) collective-permute-start(bf16[128,512]{1,0:T(8,128)(2,1)S(1)} %copy-done.26), channel_id=1, source_target_pairs={{0,8},{4,12},{8,0},{12,4},{1,9},{5,13},{9,1},{13,5},{2,10},{6,14},... | collective-permute-start | bytes 393224 | tf_op jit(solution)/shard_map/ppermute | solution.py:28
  24.3 15.3 %copy-start.11 = (bf16[128,512]{1,0:T(8,128)(2,1)}, bf16[128,512]{1,0:T(8,128)(2,1)S(1)}, u32[]{:S(2)}) copy-start(bf16[128,512]{1,0:T(8,128)(2,1)S(1)} %collective-permute-done.10.refs_13_.refs_7_) | copy-start | bytes 393220
  28.8 10.8 %copy-start.1 = (bf16[4,128,128]{2,1,0:T(8,128)(2,1)}, bf16[4,128,128]{2,1,0:T(8,128)(2,1)S(1)}, u32[]{:S(2)}) copy-start(bf16[4,128,128]{2,1,0:T(8,128)(2,1)S(1)} %all-to-all-done.1) | copy-start | bytes 393220
  28.8 5.0 %collective-permute-start.15 = (bf16[512,128]{1,0:T(8,128)(2,1)S(1)}, bf16[512,128]{1,0:T(8,128)(2,1)S(1)}, u32[]{:S(2)}, u32[]{:S(2)}) collective-permute-start(bf16[512,128]{1,0:T(8,128)(2,1)S(1)} %bitcast.13), channel_id=1, source_target_pairs={{0,8},{4,12},{8,0},{12,4},{1,9},{5,13},{9,1},{13,5},{2,10},{6,14},... | collective-permute-start | bytes 393224 | tf_op jit(solution)/shard_map/ppermute | solution.py:28
  29.3 26.3 %copy-start.9 = (bf16[128,512]{1,0:T(8,128)(2,1)}, bf16[128,512]{1,0:T(8,128)(2,1)S(1)}, u32[]{:S(2)}) copy-start(bf16[128,512]{1,0:T(8,128)(2,1)S(1)} %collective-permute-done.11.refs_14_.refs_6_) | copy-start | bytes 393220
  29.3 4.5 %collective-permute-start.16 = (bf16[512,128]{1,0:T(8,128)(2,1)S(1)}, bf16[512,128]{1,0:T(8,128)(2,1)S(1)}, u32[]{:S(2)}, u32[]{:S(2)}) collective-permute-start(bf16[512,128]{1,0:T(8,128)(2,1)S(1)} %bitcast.14), channel_id=1, source_target_pairs={{0,4},{4,0},{8,12},{12,8},{1,5},{5,1},{9,13},{13,9},{2,6},{6,2},{1... | collective-permute-start | bytes 393224 | tf_op jit(solution)/shard_map/ppermute | solution.py:28
  29.3 26.2 %copy-start.15 = (bf16[64,2048]{1,0:T(8,128)(2,1)}, bf16[64,2048]{1,0:T(8,128)(2,1)S(1)}, u32[]{:S(2)}) copy-start(bf16[64,2048]{1,0:T(8,128)(2,1)S(1)} %collective-permute-done.3.refs_6_) | copy-start | bytes 786436
  29.3 8.7 %collective-permute-start.5 = (bf16[64,2048]{1,0:T(8,128)(2,1)S(1)}, bf16[64,2048]{1,0:T(8,128)(2,1)S(1)}, u32[]{:S(2)}, u32[]{:S(2)}) collective-permute-start(bf16[64,2048]{1,0:T(8,128)(2,1)S(1)} %collective-permute-done.3.refs_6_), channel_id=1, source_target_pairs={{0,1},{1,0},{2,3},{3,2},{4,5},{5,4},{6,7},{7,6},{8,9},{9,8},{10,11... | collective-permute-start | bytes 786440 | tf_op jit(solution)/shard_map/ppermute | solution.py:31
  31.7 23.9 %copy-start.17 = (bf16[64,2048]{1,0:T(8,128)(2,1)}, bf16[64,2048]{1,0:T(8,128)(2,1)S(1)}, u32[]{:S(2)}) copy-start(bf16[64,2048]{1,0:T(8,128)(2,1)S(1)} %collective-permute-done.1.refs_4_) | copy-start | bytes 786436
  31.7 10.4 %collective-permute-start.7 = (bf16[128,1024]{1,0:T(8,128)(2,1)}, bf16[128,1024]{1,0:T(8,128)(2,1)S(1)}, u32[]{:S(2)}, u32[]{:S(2)}) collective-permute-start(bf16[128,1024]{1,0:T(8,128)(2,1)} %get-tuple-element.34), channel_id=1, source_target_pairs={{0,8},{4,12},{8,0},{12,4},{1,9},{5,13},{9,1},{13,5},{2,10},{6,14},... | collective-permute-start | bytes 786440 | tf_op jit(solution)/shard_map/ppermute | solution.py:28
  33.8 5.8 %copy-start.2 = (bf16[512,128]{1,0:T(8,128)(2,1)}, bf16[512,128]{1,0:T(8,128)(2,1)S(1)}, u32[]{:S(2)}) copy-start(bf16[512,128]{1,0:T(8,128)(2,1)S(1)} %collective-permute-done.15.refs_1_) | copy-start | bytes 393220
  33.8 9.7 %collective-permute-start.8 = (bf16[128,1024]{1,0:T(8,128)(2,1)}, bf16[128,1024]{1,0:T(8,128)(2,1)S(1)}, u32[]{:S(2)}, u32[]{:S(2)}) collective-permute-start(bf16[128,1024]{1,0:T(8,128)(2,1)} %get-tuple-element.35), channel_id=1, source_target_pairs={{0,12},{4,8},{8,4},{12,0},{1,13},{5,9},{9,5},{13,1},{2,14},{6,10},... | collective-permute-start | bytes 786440 | tf_op jit(solution)/shard_map/ppermute | solution.py:28
  33.8 5.8 %copy-start.3 = (bf16[512,128]{1,0:T(8,128)(2,1)}, bf16[512,128]{1,0:T(8,128)(2,1)S(1)}, u32[]{:S(2)}) copy-start(bf16[512,128]{1,0:T(8,128)(2,1)S(1)} %collective-permute-done.16.refs_2_) | copy-start | bytes 393220
  33.8 1.9 %collective-permute-start.17 = (bf16[512,128]{1,0:T(8,128)(2,1)S(1)}, bf16[512,128]{1,0:T(8,128)(2,1)S(1)}, u32[]{:S(2)}, u32[]{:S(2)}) collective-permute-start(bf16[512,128]{1,0:T(8,128)(2,1)S(1)} %collective-permute-done.15.refs_1_), channel_id=1, source_target_pairs={{0,4},{4,0},{8,12},{12,8},{1,5},{5,1},{9,13},{13,9},{2,6},{6,2},{1... | collective-permute-start | bytes 393224 | tf_op jit(solution)/shard_map/ppermute | solution.py:28
  35.7 14.9 %collective-permute-start.4 = (bf16[64,2048]{1,0:T(8,128)(2,1)S(1)}, bf16[64,2048]{1,0:T(8,128)(2,1)S(1)}, u32[]{:S(2)}, u32[]{:S(2)}) collective-permute-start(bf16[64,2048]{1,0:T(8,128)(2,1)S(1)} %collective-permute-done.3.refs_6_), channel_id=1, source_target_pairs={{0,16},{16,0},{1,17},{17,1},{2,18},{18,2},{3,19},{19,3},{4,20},{20... | collective-permute-start | bytes 786440 | tf_op jit(solution)/shard_map/ppermute | solution.py:34
  37.0 13.7 %collective-permute-start.2 = (bf16[64,2048]{1,0:T(8,128)(2,1)S(1)}, bf16[64,2048]{1,0:T(8,128)(2,1)S(1)}, u32[]{:S(2)}, u32[]{:S(2)}) collective-permute-start(bf16[64,2048]{1,0:T(8,128)(2,1)S(1)} %collective-permute-done.1.refs_4_), channel_id=1, source_target_pairs={{0,16},{16,0},{1,17},{17,1},{2,18},{18,2},{3,19},{19,3},{4,20},{20... | collective-permute-start | bytes 786440 | tf_op jit(solution)/shard_map/ppermute | solution.py:34
  38.0 10.7 %copy-start.18 = (bf16[64,2048]{1,0:T(8,128)(2,1)}, bf16[64,2048]{1,0:T(8,128)(2,1)S(1)}, u32[]{:S(2)}) copy-start(bf16[64,2048]{1,0:T(8,128)(2,1)S(1)} %collective-permute-done.5.refs_8_) | copy-start | bytes 786436
  38.0 17.5 %collective-permute-start.6 = (bf16[64,2048]{1,0:T(8,128)(2,1)S(1)}, bf16[64,2048]{1,0:T(8,128)(2,1)S(1)}, u32[]{:S(2)}, u32[]{:S(2)}) collective-permute-start(bf16[64,2048]{1,0:T(8,128)(2,1)S(1)} %collective-permute-done.5.refs_8_), channel_id=1, source_target_pairs={{0,16},{16,0},{1,17},{17,1},{2,18},{18,2},{3,19},{19,3},{4,20},{20... | collective-permute-start | bytes 786440 | tf_op jit(solution)/shard_map/ppermute | solution.py:34
  42.1 22.4 %collective-permute-start.20 = (bf16[256,512]{1,0:T(8,128)(2,1)}, bf16[256,512]{1,0:T(8,128)(2,1)}, u32[]{:S(2)}, u32[]{:S(2)}) collective-permute-start(bf16[256,512]{1,0:T(8,128)(2,1)} %get-tuple-element.49), channel_id=1, source_target_pairs={{0,1},{1,0},{2,3},{3,2},{4,5},{5,4},{6,7},{7,6},{8,9},{9,8},{10,11... | collective-permute-start | bytes 786440 | tf_op jit(solution)/shard_map/ppermute | solution.py:31
  43.5 5.2 %collective-permute-start.12 = (bf16[128,512]{1,0:T(8,128)(2,1)}, bf16[128,512]{1,0:T(8,128)(2,1)S(1)}, u32[]{:S(2)}, u32[]{:S(2)}) collective-permute-start(bf16[128,512]{1,0:T(8,128)(2,1)} %get-tuple-element.39), channel_id=1, source_target_pairs={{0,12},{4,8},{8,4},{12,0},{1,13},{5,9},{9,5},{13,1},{2,14},{6,10},... | collective-permute-start | bytes 393224 | tf_op jit(solution)/shard_map/ppermute | solution.py:28
  48.7 6.8 %copy-start.12 = (bf16[128,512]{1,0:T(8,128)(2,1)}, bf16[128,512]{1,0:T(8,128)(2,1)S(1)}, u32[]{:S(2)}) copy-start(bf16[128,512]{1,0:T(8,128)(2,1)S(1)} %collective-permute-done.12.refs_15_.refs_7_) | copy-start | bytes 393220
  48.7 21.6 %collective-permute-start.18 = (bf16[256,1024]{1,0:T(8,128)(2,1)}, bf16[256,1024]{1,0:T(8,128)(2,1)S(1)}, u32[]{:S(2)}, u32[]{:S(2)}) collective-permute-start(bf16[256,1024]{1,0:T(8,128)(2,1)} %get-tuple-element.46), channel_id=1, source_target_pairs={{0,1},{1,0},{2,3},{3,2},{4,5},{5,4},{6,7},{7,6},{8,9},{9,8},{10,11... | collective-permute-start | bytes 1572872 | tf_op jit(solution)/shard_map/ppermute | solution.py:31
  50.6 4.9 %copy-start.20 = (bf16[64,2048]{1,0:T(8,128)(2,1)}, bf16[64,2048]{1,0:T(8,128)(2,1)S(1)}, u32[]{:S(2)}) copy-start(bf16[64,2048]{1,0:T(8,128)(2,1)S(1)} %collective-permute-done.2.refs_5_) | copy-start | bytes 786436
  50.6 4.9 %copy-start.19 = (bf16[64,2048]{1,0:T(8,128)(2,1)}, bf16[64,2048]{1,0:T(8,128)(2,1)S(1)}, u32[]{:S(2)}) copy-start(bf16[64,2048]{1,0:T(8,128)(2,1)S(1)} %collective-permute-done.4.refs_7_) | copy-start | bytes 786436
  60.7 3.9 %copy-start.24 = (bf16[128,512]{1,0:T(8,128)(2,1)S(1)}, bf16[128,512]{1,0:T(8,128)(2,1)}, u32[]{:S(2)}) copy-start(bf16[128,512]{1,0:T(8,128)(2,1)} %get-tuple-element.50) | copy-start | bytes 393220
  60.7 8.0 %copy-start.14 = (f32[256,512]{1,0:T(8,128)S(1)}, f32[256,512]{1,0:T(8,128)}, u32[]{:S(2)}) copy-start(f32[256,512]{1,0:T(8,128)} %get-tuple-element.40) | copy-start | bytes 1572868
  60.7 8.0 %collective-permute-start.13 = (bf16[256,512]{1,0:T(8,128)(2,1)}, bf16[256,512]{1,0:T(8,128)(2,1)S(1)}, u32[]{:S(2)}, u32[]{:S(2)}) collective-permute-start(bf16[256,512]{1,0:T(8,128)(2,1)} %get-tuple-element.41), channel_id=1, source_target_pairs={{0,4},{4,0},{8,12},{12,8},{1,5},{5,1},{9,13},{13,9},{2,6},{6,2},{1... | collective-permute-start | bytes 786440 | tf_op jit(solution)/shard_map/ppermute | solution.py:28
  60.7 9.6 %copy-start.22 = (bf16[128,1024]{1,0:T(8,128)(2,1)S(1)}, bf16[128,1024]{1,0:T(8,128)(2,1)}, u32[]{:S(2)}) copy-start(bf16[128,1024]{1,0:T(8,128)(2,1)} %get-tuple-element.47) | copy-start | bytes 786436
  63.3 12.5 %copy-start.25 = (bf16[128,512]{1,0:T(8,128)(2,1)S(1)}, bf16[128,512]{1,0:T(8,128)(2,1)}, u32[]{:S(2)}) copy-start(bf16[128,512]{1,0:T(8,128)(2,1)} %get-tuple-element.53) | copy-start | bytes 393220
  63.3 29.3 %copy-start.8 = (f32[128,1024]{1,0:T(8,128)S(1)}, f32[128,1024]{1,0:T(8,128)}, u32[]{:S(2)}) copy-start(f32[128,1024]{1,0:T(8,128)} %get-tuple-element.45) | copy-start | bytes 1572868
  63.3 12.5 %collective-permute-start.22 = (bf16[256,512]{1,0:T(8,128)(2,1)}, bf16[256,512]{1,0:T(8,128)(2,1)S(1)}, u32[]{:S(2)}, u32[]{:S(2)}) collective-permute-start(bf16[256,512]{1,0:T(8,128)(2,1)} %get-tuple-element.52), channel_id=1, source_target_pairs={{0,1},{1,0},{2,3},{3,2},{4,5},{5,4},{6,7},{7,6},{8,9},{9,8},{10,11... | collective-permute-start | bytes 786440 | tf_op jit(solution)/shard_map/ppermute | solution.py:31
  65.5 27.3 %collective-permute-start.21 = (bf16[128,512]{1,0:T(8,128)(2,1)S(1)}, bf16[128,512]{1,0:T(8,128)(2,1)S(1)}, u32[]{:S(2)}, u32[]{:S(2)}) collective-permute-start(bf16[128,512]{1,0:T(8,128)(2,1)S(1)} %slice_add_fusion.3), channel_id=1, source_target_pairs={{0,2},{1,3},{2,0},{3,1},{4,6},{5,7},{6,4},{7,5},{8,10},{9,11},{10,... | collective-permute-start | bytes 393224 | tf_op jit(solution)/shard_map/ppermute | solution.py:31
  68.8 8.7 %collective-permute-start.14 = (bf16[128,512]{1,0:T(8,128)(2,1)S(1)}, bf16[128,512]{1,0:T(8,128)(2,1)S(1)}, u32[]{:S(2)}, u32[]{:S(2)}) collective-permute-start(bf16[128,512]{1,0:T(8,128)(2,1)S(1)} %slice.53), channel_id=1, source_target_pairs={{0,8},{4,12},{8,0},{12,4},{1,9},{5,13},{9,1},{13,5},{2,10},{6,14},... | collective-permute-start | bytes 393224 | tf_op jit(solution)/shard_map/ppermute | solution.py:28
  70.3 22.2 %collective-permute-start.19 = (bf16[128,1024]{1,0:T(8,128)(2,1)S(1)}, bf16[128,1024]{1,0:T(8,128)(2,1)S(1)}, u32[]{:S(2)}, u32[]{:S(2)}) collective-permute-start(bf16[128,1024]{1,0:T(8,128)(2,1)S(1)} %slice_add_fusion), channel_id=1, source_target_pairs={{0,2},{1,3},{2,0},{3,1},{4,6},{5,7},{6,4},{7,5},{8,10},{9,11},{10,... | collective-permute-start | bytes 786440 | tf_op jit(solution)/shard_map/ppermute | solution.py:31
  75.8 17.0 %copy-start.16 = (f32[128,512]{1,0:T(8,128)S(1)}, f32[128,512]{1,0:T(8,128)}, u32[]{:S(2)}) copy-start(f32[128,512]{1,0:T(8,128)} %get-tuple-element.48) | copy-start | bytes 786436
  75.8 19.5 %collective-permute-start.23 = (bf16[128,512]{1,0:T(8,128)(2,1)S(1)}, bf16[128,512]{1,0:T(8,128)(2,1)S(1)}, u32[]{:S(2)}, u32[]{:S(2)}) collective-permute-start(bf16[128,512]{1,0:T(8,128)(2,1)S(1)} %slice_add_fusion.2), channel_id=1, source_target_pairs={{0,2},{1,3},{2,0},{3,1},{4,6},{5,7},{6,4},{7,5},{8,10},{9,11},{10,... | collective-permute-start | bytes 393224 | tf_op jit(solution)/shard_map/ppermute | solution.py:31
  78.1 17.2 %copy-start.23 = (f32[128,512]{1,0:T(8,128)S(1)}, f32[128,512]{1,0:T(8,128)}, u32[]{:S(2)}) copy-start(f32[128,512]{1,0:T(8,128)} %get-tuple-element.51) | copy-start | bytes 786436
  78.1 17.9 %all-to-all-start = ((bf16[4,128,128]{2,1,0:T(8,128)(2,1)}), bf16[4,128,128]{2,1,0:T(8,128)(2,1)S(1)}, u32[]{:S(2)}, u32[]{:S(2)}) async-start(bf16[4,128,128]{2,1,0:T(8,128)(2,1)} %bitcast_bitcast_fusion), calls=%async_computation | async-start | bytes 262144 | tf_op jit(solution)/shard_map/all_to_all | solution.py:318
  95.3 4.4 %copy-start.5 = (f32[128,2048]{1,0:T(8,128)}, f32[128,2048]{1,0:T(8,128)S(1)}, u32[]{:S(2)}) copy-start(f32[128,2048]{1,0:T(8,128)S(1)} %add_dynamic-update-slice_fusion) | copy-start | bytes 3145732
  (6 other events, 13.5 us)
